TPU v7x, 32 devices: a whole 2x2x4 slice. The times are simulated.
32 devices in a mesh: groups: 2 (over x), ep: 16 (over z, y, core).
Axes of the slice: x: 2, y: 2, z: 4, core: 2. Of those that a mesh axis runs over, the one named last changes fastest.
Arguments:
- residual: bfloat16 [2048, 7168], P('groups', 'ep'), parts along dimension 0, may hold values from -6 to 6
- attn_out: bfloat16 [2048, 7168], P('groups', 'ep'), parts along dimension 0, may hold values from -6 to 6
- norm_gain: float32 [7168], replicated, may hold values from 0.5 to 1.5
- expert_routes: int32 [2048, 2], P(('groups', 'ep')), parts along dimension 0, may hold values from 0 to 2, as said below
- route_gain: float32 [2048, 2], P(('groups', 'ep')), parts along dimension 0, may hold values from 0.1 to 1
- w_gate: bfloat16 [7168, 4096], P(None, 'ep'), may hold values from -0.0625 to 0.0625
- w_up: bfloat16 [7168, 4096], P(None, 'ep'), may hold values from -0.0625 to 0.0625
- w_down: bfloat16 [4096, 7168], P('ep'), may hold values from -0.125 to 0.125
Outputs:
- mixed: bfloat16 [2048, 7168], P(('groups', 'ep')), parts along dimension 0
There are 2 independent parts, one for each index of `groups`. A program takes and returns all parts, laid end to end along the dimension named above; an argument that names none is the same for every part. Nothing has to cross between parts.
Inputs may be any that keep to these rules, and one draw needn't show every extreme that they name: `expert_routes`: value 2 marks a route to an expert outside this wave; a token names each expert of the wave at most once. Among the tokens of one block of 64, at most 64 routes name one expert, and in every draw some expert is named exactly 64 times by every block.
All inputs are finite; a program needn't handle non-finite values.
Results may differ from a plain program's by a relative error of at most 0.0055.
Values may be sent and summed in bfloat16 or wider, within the bound.
A program may use at most 192 MiB of HBM per device.

v0:
```python
import jax
import jax.numpy as jnp
from jax import lax
from jax.sharding import PartitionSpec as P

FSPLIT = 8


epsilon = 1e-06


def normalize(stream_rows, norm_gain):
    values = stream_rows.astype(jnp.float32)
    inv_rms = lax.rsqrt(jnp.mean(values * values, axis=-1, keepdims=True) + epsilon)
    return (values * inv_rms * norm_gain).astype(jnp.bfloat16)


def route_match(routes, experts, capacity):
    flat_ids = routes.reshape(-1)
    onehot = (flat_ids[:, None] == jnp.arange(experts, dtype=jnp.int32)[None, :]).astype(jnp.int32)
    earlier = jnp.cumsum(onehot, axis=0) - onehot
    slot_pos = jnp.sum(earlier * onehot, axis=1)
    slot_code = jnp.where(flat_ids < experts, flat_ids * capacity + slot_pos, -1)
    target = jnp.arange(experts * capacity, dtype=jnp.int32)
    return slot_code[None, :] == target[:, None]


def selection(routes, experts, capacity):
    matched = route_match(routes, experts, capacity).astype(jnp.int32)
    return matched.reshape(experts * capacity, routes.shape[0], routes.shape[1]).sum(axis=2)


def gain_table(routes, route_gain, experts, capacity):
    matched = route_match(routes, experts, capacity)
    weighted = jnp.where(matched, route_gain.reshape(-1)[None, :], 0.0)
    return weighted.reshape(experts * capacity, routes.shape[0], routes.shape[1]).sum(axis=2).T


def expert_rows(normed, w_gate, w_up, w_down):
    gate_act = jnp.dot(normed, w_gate, preferred_element_type=jnp.float32)
    up_act = jnp.dot(normed, w_up, preferred_element_type=jnp.float32)
    hidden = (jax.nn.silu(gate_act) * up_act).astype(jnp.bfloat16)
    return jnp.dot(hidden, w_down, preferred_element_type=jnp.float32).astype(jnp.bfloat16)


def body(residual, attn_out, norm_gain, expert_routes, route_gain, w_gate, w_up, w_down):
    devices = lax.axis_size("ep")
    tok_here = expert_routes.shape[0]
    route_slots = expert_routes.shape[1]
    experts = devices // FSPLIT
    capacity = route_slots * tok_here // experts
    model_width = w_gate.shape[0]
    stream_feat = (residual.astype(jnp.float32) + attn_out.astype(jnp.float32)).astype(jnp.bfloat16)
    stream_rows = lax.all_to_all(stream_feat, "ep", split_axis=0, concat_axis=1, tiled=True)
    combine_weights = gain_table(expert_routes, route_gain, experts, capacity)
    normed_rows = normalize(stream_rows, norm_gain)
    select = selection(expert_routes, experts, capacity).astype(jnp.bfloat16)
    per_expert = jnp.dot(select, normed_rows, preferred_element_type=jnp.float32).astype(
        jnp.bfloat16
    )
    per_expert = per_expert.reshape(experts, 1, capacity, model_width)
    outgoing = jnp.broadcast_to(per_expert, (experts, FSPLIT, capacity, model_width))
    outgoing = outgoing.reshape(devices, capacity, model_width)
    received = lax.all_to_all(outgoing, "ep", split_axis=0, concat_axis=0, tiled=True)
    slot_count = received.shape[1]
    partial_value = expert_rows(received.reshape(-1, model_width), w_gate, w_up, w_down)
    partial_value = partial_value.reshape(devices, slot_count, model_width)
    returned = lax.all_to_all(partial_value, "ep", split_axis=0, concat_axis=0, tiled=True)
    summed = (
        returned.reshape(experts, FSPLIT, capacity, model_width).astype(jnp.float32).sum(axis=1)
    )
    summed = summed.reshape(experts * capacity, model_width)
    routed_sum = jnp.dot(combine_weights, summed, precision=lax.Precision.HIGHEST)
    return (stream_rows.astype(jnp.float32) + routed_sum).astype(jnp.bfloat16)


def solution(mesh):
    in_specs = (
        P("groups", "ep"),
        P("groups", "ep"),
        P(),
        P(("groups", "ep"), None),
        P(("groups", "ep"), None),
        P(None, "ep"),
        P(None, "ep"),
        P("ep", None),
    )
    out_specs = P(("groups", "ep"), None)
    return jax.shard_map(body, mesh=mesh, in_specs=in_specs, out_specs=out_specs, check_vma=False)
```

profile of v0, /device:TPU:13, one launch (start us, length us, event | category | flops | bytes accessed | tf_op | source)
XLA Modules:
  0.0 732.1 jit_solution(11290937489123675443)
XLA Ops:
  0.0 0.0 copy-start.2
  0.0 1.8 add_convert_fusion
  1.8 1.3 copy.34
  3.1 6.5 all-to-all-start
  9.7 0.0 copy-done.2
  9.7 0.1 copy.36
  9.8 0.1 eq.16
  9.9 0.1 fusion.11
  10.0 0.2 reduce_window_sum.12
  10.2 0.2 select_reduce_fusion.1
  10.4 0.1 reduce_sum.52
  10.5 0.1 copy.37
  10.6 0.1 convert_reduce_fusion.1
  10.7 23.8 %all-to-all-done = bf16[16,64,448]{2,1,0:T(8,128)(2,1)S(1)} async-done(((bf16[16,64,448]{2,1,0:T(8,128)(2,1)}), bf16[16,64,448]{2,1,0:T(8,128)(2,1)S(1)}, u32[]{:S(2)}, u32[]{:S(2)}) %all-to-all-start) | async-done | bytes 917536 | tf_op jit(solution)/shard_map/all_to_all | solution.py:54
  34.5 0.3 convert_bitcast_fusion
  34.8 0.0 copy-start.1
  34.8 2.6 copy.35
  37.4 2.2 reshape.74
  39.6 0.3 fusion.1
  39.9 0.0 copy-done.1
  39.9 0.7 convolution_convert_fusion.1
  40.6 1.9 broadcast_in_dim.36
  42.5 0.0 copy-start.4
  42.5 321.8 %all_to_all.23 = bf16[16,64,7168]{2,1,0:T(8,128)(2,1)S(1)} all-to-all(bf16[16,64,7168]{2,1,0:T(8,128)(2,1)S(1)} %bitcast.21), channel_id=1, replica_groups=mesh['groups'=2,'ep'=16] {'ep'}, dimensions={0} | all-to-all | bytes 29360128 | tf_op jit(solution)/shard_map/all_to_all | solution.py:64
  364.4 0.0 copy-start
  364.4 5.2 copy-done
  369.6 0.0 copy-done.4
  369.6 3.9 fusion.14
  373.5 23.7 %convolution_convert_fusion = bf16[1024,7168]{1,0:T(8,128)(2,1)} fusion(bf16[256,7168]{1,0:T(8,128)(2,1)} %param.15, bf16[1024,7168]{1,0:T(8,128)(2,1)} %bitcast.20, bf16[7168,256]{1,0:T(8,128)(2,1)} %param.14, f32[1024,256]{1,0:T(8,128)S(1)} %fusion.14), kind=kOutput, calls=%fused_computation.1 | convolution fusion | flops 7525105664 | bytes 37748736 | tf_op jit(solution)/shard_map/dot_general | solution.py:43
  397.2 0.0 copy-start.3
  397.2 6.3 all-to-all-start.2
  403.6 0.0 copy-done.3
  403.6 0.1 select_reduce_fusion
  403.7 317.1 %all-to-all-done.2 = bf16[16,64,7168]{2,1,0:T(8,128)(2,1)} async-done(((bf16[16,64,7168]{2,1,0:T(8,128)(2,1)}), bf16[16,64,7168]{2,1,0:T(8,128)(2,1)}, u32[]{:S(2)}, u32[]{:S(2)}) %all-to-all-start.2) | async-done | bytes 14680096 | tf_op jit(solution)/shard_map/all_to_all | solution.py:68
  720.7 8.4 %convert_reduce_fusion = f32[2,64,7168]{2,1,0:T(8,128)S(1)} fusion(bf16[16,64,7168]{2,1,0:T(8,128)(2,1)} %all-to-all-done.2), kind=kLoop, calls=%fused_computation | loop fusion | flops 13762560 | bytes 18350080 | tf_op jit(solution)/shard_map/reduce_sum | solution.py:70
  729.1 3.0 fusion
  (2 shorter events, 0.0 us)
Async XLA Ops:
  0.0 9.7 %copy-start.2 = (s32[64,2]{0,1:T(2,128)S(1)}, s32[64,2]{0,1:T(2,128)}, u32[]{:S(2)}) copy-start(s32[64,2]{0,1:T(2,128)} %param.11) | copy-start | bytes 1540
  3.1 31.4 %all-to-all-start = ((bf16[16,64,448]{2,1,0:T(8,128)(2,1)}), bf16[16,64,448]{2,1,0:T(8,128)(2,1)S(1)}, u32[]{:S(2)}, u32[]{:S(2)}) async-start(bf16[16,64,448]{2,1,0:T(8,128)(2,1)} %bitcast), calls=%async_computation | async-start | bytes 2097152 | tf_op jit(solution)/shard_map/all_to_all | solution.py:54
  34.8 5.1 copy-start.1
  42.5 327.0 %copy-start.4 = (bf16[7168,256]{1,0:T(8,128)(2,1)S(1)}, bf16[7168,256]{1,0:T(8,128)(2,1)}, u32[]{:S(2)}) copy-start(bf16[7168,256]{1,0:T(8,128)(2,1)} %param.13) | copy-start | bytes 11010052
  364.4 5.2 copy-start
  397.2 6.3 copy-start.3
  397.2 323.5 %all-to-all-start.2 = ((bf16[16,64,7168]{2,1,0:T(8,128)(2,1)}), bf16[16,64,7168]{2,1,0:T(8,128)(2,1)}, u32[]{:S(2)}, u32[]{:S(2)}) async-start(bf16[16,64,7168]{2,1,0:T(8,128)(2,1)} %bitcast.18), calls=%async_computation.2 | async-start | bytes 29360128 | tf_op jit(solution)/shard_map/all_to_all | solution.py:68
where the time goes:
time: 733 us; the launch traced here: 732 us
  waiting for transfers between devices  341 us (47%)
  blocking collectives  322 us (44%)
  matrix products  31.3 us (4%)
  local copies, waits for them, and re-layouts  13.6 us (2%)
  starting transfers between devices  12.9 us (2%)
  other arithmetic  11.5 us (2%)
    all_to_all x1, blocking collectives, body(): lax.all_to_all(outgoing, 'ep', split_axis=0, concat_axis=0, tiled=True)  322 us
    all_to_all x1, waiting for transfers between devices, body(): lax.all_to_all(partial_value, 'ep', split_axis=0, concat_axis=0, tiled=True)  317 us
    all_to_all x1, waiting for transfers between devices, body(): lax.all_to_all(stream_feat, 'ep', split_axis=0, concat_axis=1, tiled=True)  23.8 us
    dot_general x1, matrix products, expert_rows(): jnp.dot(hidden, w_down, preferred_element_type=jnp.float32)  23.7 us
  transfers between devices with their start and end apart: 2, of which 2 were waited for; matrix products, arithmetic and copies ran while one was open for 0% of the time, Pallas kernels for 0%

commit v1 on v0

--- a/solution.py
+++ b/solution.py
@@ -74,6 +74,37 @@
     return (stream_rows.astype(jnp.float32) + routed_sum).astype(jnp.bfloat16)
 
 
+def dense_body(residual, attn_out, norm_gain, expert_routes, route_gain, w_gate, w_up, w_down):
+    devices = lax.axis_size("ep")
+    rank = lax.axis_index("ep")
+    tok_here = expert_routes.shape[0]
+    experts = devices // FSPLIT
+    stream_feat = (residual.astype(jnp.float32) + attn_out.astype(jnp.float32)).astype(jnp.bfloat16)
+    named = jnp.arange(experts, dtype=jnp.int32)
+    gains = jnp.sum(
+        jnp.where(expert_routes[:, :, None] == named, route_gain[:, :, None], 0.0), axis=1
+    )
+    all_gains = lax.all_gather(gains, "ep", axis=0, tiled=True)
+    here = (rank // FSPLIT == named).astype(jnp.float32)
+    gain_here = jnp.sum(all_gains * here, axis=1, keepdims=True)
+    stream = lax.all_gather(stream_feat, "ep", axis=1, tiled=True)
+    normed = normalize(stream, norm_gain)
+    gate_act = jnp.dot(normed, w_gate, preferred_element_type=jnp.float32)
+    up_act = jnp.dot(normed, w_up, preferred_element_type=jnp.float32)
+    hidden = (jax.nn.silu(gate_act) * up_act * gain_here).astype(jnp.bfloat16)
+    partial = jnp.dot(hidden, w_down, preferred_element_type=jnp.float32).astype(jnp.bfloat16)
+    routed = lax.psum_scatter(partial, "ep", scatter_dimension=0, tiled=True)
+    own = lax.dynamic_slice_in_dim(stream, rank * tok_here, tok_here, 0)
+    return (own.astype(jnp.float32) + routed.astype(jnp.float32)).astype(jnp.bfloat16)
+
+
+def pick_body(residual, attn_out, norm_gain, expert_routes, route_gain, w_gate, w_up, w_down):
+    experts = lax.axis_size("ep") // FSPLIT
+    capacity = expert_routes.shape[1] * expert_routes.shape[0] // experts
+    run = dense_body if capacity >= expert_routes.shape[0] else body
+    return run(residual, attn_out, norm_gain, expert_routes, route_gain, w_gate, w_up, w_down)
+
+
 def solution(mesh):
     in_specs = (
         P("groups", "ep"),
@@ -86,4 +117,4 @@
         P("ep", None),
     )
     out_specs = P(("groups", "ep"), None)
-    return jax.shard_map(body, mesh=mesh, in_specs=in_specs, out_specs=out_specs, check_vma=False)
+    return jax.shard_map(pick_body, mesh=mesh, in_specs=in_specs, out_specs=out_specs, check_vma=False)

time: 733 us -> 323 us (0.44)
  blocking collectives: 322 us -> 15.8 us
  waiting for transfers between devices: 341 us -> 242 us
  between operations: 0.13 us -> 13.5 us
  starting transfers between devices: 12.9 us -> 0.04 us
  local copies, waits for them, and re-layouts: 13.6 us -> 2.91 us
    all_to_all x2 -> x0, waiting for transfers between devices: 341 us -> none  [the longest x1 317 us: body(): lax.all_to_all(partial_value, 'ep', split_axis=0, concat_axis=0, tiled=True)]
    all_to_all x1 -> x0, blocking collectives: 322 us -> none  [body(): lax.all_to_all(outgoing, 'ep', split_axis=0, concat_axis=0, tiled=True)]
    reduce_scatter x0 -> x1, waiting for transfers between devices: none -> 146 us  [dense_body(): routed = lax.psum_scatter(partial, 'ep', scatter_dimension=0, tiled=True)]
    all_gather x0 -> x1, waiting for transfers between devices: none -> 96.2 us  [dense_body(): stream = lax.all_gather(stream_feat, 'ep', axis=1, tiled=True)]
    all_gather x0 -> x1, blocking collectives: none -> 15.8 us  [dense_body(): all_gains = lax.all_gather(gains, 'ep', axis=0, tiled=True)]
    all_to_all x2 -> x0, starting transfers between devices: 12.9 us -> none  [the longest x1 6.52 us: body(): lax.all_to_all(stream_feat, 'ep', split_axis=0, concat_axis=1, tiled=True)]
    reduce_sum x4 -> x2, other arithmetic: 8.77 us -> 0.79 us  [the longest x1 0.71 us: dense_body(): jnp.sum(jnp.where(expert_routes[:, :, None] == named, route_gain[:, :, No...]
    reduce_sum x1, other arithmetic: 0.32 us -> 8.08 us  [normalize(): jnp.mean(values * values, axis=-1, keepdims=True) + epsilon]
  transfers between devices with their start and end apart: 2 -> 2, of which waited for: 2 -> 2; matrix products, arithmetic and copies ran while one was open for 0% -> 1% of each run, Pallas kernels for 0% -> 0%
where the time goes in v1:
time: 323 us; the launch traced here: 320 us
  waiting for transfers between devices  242 us (75%)
  matrix products  31.3 us (10%)
  blocking collectives  15.8 us (5%)
  other arithmetic  13.9 us (4%)
  between operations  13.5 us (4%)
    reduce_scatter x1, waiting for transfers between devices, dense_body(): routed = lax.psum_scatter(partial, 'ep', scatter_dimension=0, tiled=True)  146 us
    all_gather x1, waiting for transfers between devices, dense_body(): stream = lax.all_gather(stream_feat, 'ep', axis=1, tiled=True)  96.2 us
    all_gather x1, blocking collectives, dense_body(): all_gains = lax.all_gather(gains, 'ep', axis=0, tiled=True)  15.8 us
    dot_general x1, matrix products, dense_body(): gate_act = jnp.dot(normed, w_gate, preferred_element_type=jnp.float32)  12.8 us
    dot_general x1, matrix products, dense_body(): jnp.dot(hidden, w_down, preferred_element_type=jnp.float32)  9.34 us
    dot_general x1, matrix products, dense_body(): up_act = jnp.dot(normed, w_up, preferred_element_type=jnp.float32)  9.16 us
    reduce_sum x1, other arithmetic, normalize(): jnp.mean(values * values, axis=-1, keepdims=True) + epsilon  8.08 us
  transfers between devices with their start and end apart: 2, of which 2 were waited for; matrix products, arithmetic and copies ran while one was open for 1% of the time, Pallas kernels for 0%

profile of v1, /device:TPU:13, one launch (start us, length us, event | category | flops | bytes accessed | tf_op | source)
XLA Modules:
  0.0 319.9 jit_solution(7956764136521179954)
XLA Ops:
  6.5 0.0 copy-start.1
  6.5 0.0 all-gather.3.cloned.1.call-start
  6.5 2.7 add_convert_fusion.1
  9.3 0.0 all-gather.3.cloned.1.call-update
  9.3 0.0 reduce-scatter.2.cloned.1.call-start
  9.4 0.7 fusion.23
  10.1 15.8 %all-gather = f32[16,64,2]{1,2,0:T(2,128)S(1)} all-gather(f32[1,64,2]{1,2,0:T(2,128)S(1)} %bitcast.11), channel_id=1, replica_groups=mesh['groups'=2,'ep'=16] {'ep'}, dimensions={0}, use_global_device_ids=true | all-gather | bytes 8704 | tf_op jit(solution)/shard_map/all_gather | solution.py:87
  25.9 0.1 reshape.18
  26.0 0.1 multiply_reduce_fusion
  26.0 96.2 %all-gather.3.cloned.1.call-done = bf16[1024,7168]{0,1:T(8,128)(2,1)} async-done(((bf16[1024,448]{0,1:T(8,128)(2,1)}), bf16[1024,7168]{0,1:T(8,128)(2,1)}) %all-gather.3.cloned.1.call-update) | async-done | bytes 14680080 | tf_op jit(solution)/shard_map/all_gather | solution.py:90
  122.3 8.1 %fusion = f32[1024]{0:T(1024)S(1)} fusion(bf16[1024,7168]{0,1:T(8,128)(2,1)} %all-gather.3.cloned.1.call-done), kind=kLoop, calls=%fused_computation.2 | loop fusion | flops 22019072 | bytes 14684160 | tf_op jit(solution)/shard_map/reduce_sum | solution.py:14
  130.3 0.0 copy-done.1
  130.4 0.0 copy-start
  130.4 12.8 %fusion.5 = f32[1024,256]{1,0:T(8,128)} fusion(bf16[7168,256]{1,0:T(8,128)(2,1)} %param.13, bf16[1024,7168]{0,1:T(8,128)(2,1)} %all-gather.3.cloned.1.call-done, f32[7168]{0:T(1024)S(1)} %copy-done.1, f32[1024]{0:T(1024)S(1)} %add_rsqrt_fusion), kind=kOutput, calls=%fused_computation.7 | convolution fusion | flops 3787456512 | bytes 19431424 | tf_op jit(solution)/shard_map/dot_general | solution.py:92
  143.1 0.0 copy-done
  143.1 9.2 %fusion.13.clone.4 = bf16[1024,256]{1,0:T(8,128)(2,1)S(1)} fusion(bf16[7168,256]{1,0:T(8,128)(2,1)} %param.14, bf16[1024,7168]{0,1:T(8,128)(2,1)S(1)} %copy-done, f32[7168]{0:T(1024)S(1)} %copy-done.1, f32[1024]{0:T(1024)S(1)} %add_rsqrt_fusion, f32[1024,256]{1,0:T(8,128)} %fusion.5, f32[1024]{0:T(1024)S(1)} %multiply_reduce_fusion), kind=kOutput, calls=%fused_computation.12.clone.clone.clone.1 | convolution fusion | flops 3789291520 | bytes 19959808 | tf_op jit(solution)/shard_map/dot_general | solution.py:93
  152.3 9.3 %convolution_convert_fusion = bf16[1024,7168]{1,0:T(8,128)(2,1)} fusion(bf16[256,7168]{1,0:T(8,128)(2,1)} %param.15, bf16[1024,256]{1,0:T(8,128)(2,1)S(1)} %fusion.13.clone.4), kind=kOutput, calls=%fused_computation.5 | convolution fusion | flops 3765436416 | bytes 18874368 | tf_op jit(solution)/shard_map/dot_general | solution.py:95
  161.7 0.0 reduce-scatter.2.cloned.1.call-update
  161.7 2.1 constant_dynamic-slice_fusion
  163.8 0.8 copy.24
  164.5 146.2 %reduce-scatter.2.cloned.1.call-done = bf16[64,7168]{1,0:T(8,128)(2,1)} async-done(((bf16[1024,7168]{1,0:T(8,128)(2,1)}), bf16[64,7168]{1,0:T(8,128)(2,1)}) %reduce-scatter.2.cloned.1.call-update) | async-done | bytes 917520 | tf_op jit(solution)/shard_map/reduce_scatter | solution.py:96
  310.8 2.3 add_convert_fusion
  (3 shorter events, 0.0 us)
Async XLA Ops:
  6.5 123.8 %copy-start.1 = (f32[7168]{0:T(1024)S(1)}, f32[7168]{0:T(1024)}, u32[]{:S(2)}) copy-start(f32[7168]{0:T(1024)} %param.10) | copy-start | bytes 86020
  6.5 115.7 %all-gather.3.cloned.1.call-start = ((), (), s32[]{:S(2)}) async-start(), calls=%async_computation.1 | async-start | bytes 15597568 | tf_op jit(solution)/shard_map/all_gather | solution.py:90
  9.3 301.5 %reduce-scatter.2.cloned.1.call-start = ((), (), s32[]{:S(2)}) async-start(), calls=%async_computation.2 | async-start | bytes 15597568 | tf_op jit(solution)/shard_map/reduce_scatter | solution.py:96
  130.4 12.8 %copy-start = (bf16[1024,7168]{0,1:T(8,128)(2,1)S(1)}, bf16[1024,7168]{0,1:T(8,128)(2,1)}, u32[]{:S(2)}) copy-start(bf16[1024,7168]{0,1:T(8,128)(2,1)} %all-gather.3.cloned.1.call-done) | copy-start | bytes 44040196
Sparse Core Ops, SparseCore 0:
  9.6 112.5 all-gather.2
  161.8 148.9 reduce-scatter.1
